TPU v7x, 256 devices: a whole 4x4x8 slice. The times are simulated.
256 devices in a mesh: dp: 16 (over z, core), vocab: 16 (over x, y).
Axes of the slice: x: 4, y: 4, z: 8, core: 2. Of those that a mesh axis runs over, the one named last changes fastest.
Arguments:
- hidden: bfloat16 [4096, 4096], P('dp')
- table: bfloat16 [16384, 4096], P(('vocab', 'dp')), as said below
- targets: int32 [4096], P('dp'), may hold values from 0 to 16383
- token_scale: float32 [4096], P('dp'), may hold values from 2 to 32
- enc_ids: int32 [4096], P(('dp', 'vocab')), may hold values from 0 to 16383
- enc_cot: bfloat16 [4096, 4096], P(('dp', 'vocab')), may hold values from -6 to 6
- dec_ids: int32 [4096], P(('dp', 'vocab')), may hold values from 0 to 16383
- dec_cot: bfloat16 [4096, 4096], P(('dp', 'vocab')), may hold values from -6 to 6
Outputs:
- grad_hidden: bfloat16 [4096, 4096], P('dp', 'vocab')
- grad_table: float32 [16384, 4096], P(('vocab', 'dp'))
- loss: float32 [4096], P('dp')
Inputs may be any that keep to these rules, and one draw needn't show every extreme that they name: table entries of order 3 / sqrt(4096).
All inputs are finite; a program needn't handle non-finite values.
Results may differ from a plain program's by a relative error of at most 0.018.
Values may be sent and summed in bfloat16 or wider, within the bound.
No kernel may reach another device: no remote copies, remote signals or barrier semaphores. Data moves between devices by JAX's collectives and lax.ppermute only.
A program may use at most 128 MiB of HBM per device.

v0:
```python
import jax
import jax.numpy as jnp
from jax import lax
from jax.sharding import PartitionSpec as P


def shards(hidden, table, targets, token_scale, enc_ids, enc_cot, dec_ids, dec_cot):
    vocab_rows = table.shape[0] * lax.axis_size("dp")
    offset = lax.axis_index("vocab") * vocab_rows
    gathered = lax.all_gather(table, "dp", axis=0, tiled=True)
    logits = jnp.dot(hidden, gathered.T, preferred_element_type=jnp.float32)
    local_target = targets - offset
    columns = jnp.arange(vocab_rows, dtype=jnp.int32)
    matches = columns[None, :] == local_target[:, None]
    target_part = jnp.sum(jnp.where(matches, logits, 0.0), axis=1)
    local_max = jnp.max(logits, axis=1)
    row_max = lax.pmax(local_max, "vocab")
    expo = jnp.exp(logits - row_max[:, None])
    row_sum, target_logit = lax.psum((jnp.sum(expo, axis=1), target_part), "vocab")
    loss = row_max + jnp.log(row_sum) - target_logit
    dlogits = (
        token_scale[:, None] * (expo / row_sum[:, None] - matches.astype(jnp.float32))
    ).astype(jnp.bfloat16)
    state_term = jnp.dot(dlogits, gathered, preferred_element_type=jnp.float32)
    grad_hidden = lax.psum_scatter(
        state_term.astype(jnp.bfloat16), "vocab", scatter_dimension=1, tiled=True
    )
    ids_one, cot_one, ids_two, cot_two = (
        lax.all_gather(enc_ids, "vocab", axis=0, tiled=True),
        lax.all_gather(enc_cot, "vocab", axis=0, tiled=True),
        lax.all_gather(dec_ids, "vocab", axis=0, tiled=True),
        lax.all_gather(dec_cot, "vocab", axis=0, tiled=True),
    )
    all_ids = jnp.concatenate([ids_one, ids_two], axis=0) - offset
    all_cot = jnp.concatenate([cot_one, cot_two], axis=0)
    hits = (columns[:, None] == all_ids[None, :]).astype(jnp.bfloat16)
    looked_up = jnp.dot(hits, all_cot, preferred_element_type=jnp.float32)
    head = lax.dot_general(
        dlogits, hidden, (((0,), (0,)), ((), ())), preferred_element_type=jnp.float32
    )
    grad_table = lax.psum_scatter(
        (head + looked_up).astype(jnp.bfloat16), "dp", scatter_dimension=0, tiled=True
    ).astype(jnp.float32)
    return (grad_hidden, grad_table, loss)


def solution(mesh):
    placed = (
        P("dp", None),
        P(("vocab", "dp"), None),
        P("dp"),
        P("dp"),
        P(("dp", "vocab")),
        P(("dp", "vocab"), None),
        P(("dp", "vocab")),
        P(("dp", "vocab"), None),
    )
    return jax.shard_map(
        shards,
        mesh=mesh,
        in_specs=placed,
        out_specs=(P("dp", "vocab"), P(("vocab", "dp"), None), P("dp")),
        check_vma=False,
    )
```

profile of v0, /device:TPU:32, one launch (start us, length us, event | category | flops | bytes accessed | tf_op | source)
XLA Modules:
  0.0 417.9 jit_solution(18154777926044538096)
XLA Ops:
  7.2 0.0 copy-start
  7.2 0.0 all-gather.6.cloned.1.call-start
  7.2 0.7 all-gather.6.cloned.1.call-update
  7.9 0.0 all-gather.8.cloned.1.call-start
  8.0 0.7 all-gather.8.cloned.1.call-update
  8.7 0.0 all-gather.4.cloned.1.call-start
  8.7 0.7 all-gather.4.cloned.1.call-update
  9.4 0.0 reduce-scatter.5.cloned.1.call-start
  9.4 1.3 dynamic-slice
  11.4 0.9 dynamic-update-slice.1
  12.2 0.8 dynamic-update-slice
  13.1 16.5 %all-reduce.2 = (s32[256]{0:T(256)S(1)}, s32[256]{0:T(256)S(1)}) all-reduce(s32[256]{0:T(256)S(1)} %dynamic-update-slice.1, s32[256]{0:T(256)S(1)} %dynamic-update-slice), channel_id=1, replica_groups=mesh['dp'=16,'vocab'=16] {'vocab'}, use_global_device_ids=true, to_apply=%add.1 | all-reduce | flops 512 | bytes 4096
  29.5 0.7 broadcast_subtract_fusion
  30.2 32.8 %all-gather.6.cloned.1.call-done = bf16[256,4096]{1,0:T(8,128)(2,1)} async-done(((bf16[16,4096]{1,0:T(8,128)(2,1)}), bf16[256,4096]{1,0:T(8,128)(2,1)}) %all-gather.6.cloned.1.call-update) | async-done | bytes 2097168 | tf_op jit(solution)/shard_map/all_gather | solution.py:30
  63.0 51.8 %all-gather.8.cloned.1.call-done = bf16[256,4096]{1,0:T(8,128)(2,1)} async-done(((bf16[16,4096]{1,0:T(8,128)(2,1)}), bf16[256,4096]{1,0:T(8,128)(2,1)}) %all-gather.8.cloned.1.call-update) | async-done | bytes 2097168 | tf_op jit(solution)/shard_map/all_gather | solution.py:32
  114.8 10.3 %fusion = f32[1024,4096]{1,0:T(8,128)} fusion(bf16[256,4096]{1,0:T(8,128)(2,1)} %all-gather.8.cloned.1.call-done, bf16[256,4096]{1,0:T(8,128)(2,1)} %all-gather.6.cloned.1.call-done, s32[512]{0:T(512)S(1)} %add_subtract_fusion), kind=kOutput, calls=%fused_computation.2 | convolution fusion | flops 4303880192 | bytes 20973568 | tf_op jit(solution)/shard_map/dot_general | solution.py:37
  125.1 45.1 %all-gather.4.cloned.1.call-done = bf16[1024,4096]{1,0:T(8,128)(2,1)} async-done(((bf16[64,4096]{1,0:T(8,128)(2,1)}), bf16[1024,4096]{1,0:T(8,128)(2,1)}) %all-gather.4.cloned.1.call-update) | async-done | bytes 8388624 | tf_op jit(solution)/shard_map/all_gather | solution.py:10
  170.2 0.0 copy-done
  170.2 5.8 %fusion.7 = (f32[256]{0:T(256)S(1)}, f32[256,1024]{1,0:T(8,128)S(1)}) fusion(bf16[256,4096]{1,0:T(8,128)(2,1)S(1)} %copy-done, bf16[1024,4096]{1,0:T(8,128)(2,1)} %all-gather.4.cloned.1.call-done), kind=kOutput, calls=%fused_computation.17 | convolution fusion | flops 2147745536 | bytes 11535360 | tf_op jit(solution)/shard_map/dot_general | solution.py:11
  176.0 40.3 %pmax.7 = f32[256]{0:T(256)S(1)} all-reduce(f32[256]{0:T(256)S(1)} %get-tuple-element.9), channel_id=1, replica_groups=mesh['dp'=16,'vocab'=16] {'vocab'}, use_global_device_ids=true, to_apply=%region_1.2 | all-reduce | flops 256 | bytes 2048 | tf_op jit(solution)/shard_map/pmax | solution.py:17
  216.4 0.5 select_reduce_fusion
  216.8 35.5 %all-reduce.3 = (f32[256]{0:T(256)S(1)}, f32[256]{0:T(256)S(1)}) all-reduce(f32[256]{0:T(256)S(1)} %get-tuple-element.4, f32[256]{0:T(256)S(1)} %get-tuple-element.3), channel_id=1, replica_groups=mesh['dp'=16,'vocab'=16] {'vocab'}, use_global_device_ids=true, to_apply=%region_3.4 | all-reduce | flops 512 | bytes 4096 | tf_op jit(solution)/shard_map/psum | solution.py:19
  252.3 0.0 copy-done.1
  252.3 9.2 %add_convert_fusion = bf16[1024,4096]{1,0:T(8,128)(2,1)} fusion(f32[1024,4096]{1,0:T(8,128)} %fusion, bf16[256,4096]{1,0:T(8,128)(2,1)S(1)} %copy-done, f32[256,1024]{1,0:T(8,128)S(1)} %get-tuple-element.10, s32[256]{0:T(256)S(1)} %broadcast_subtract_fusion, f32[256]{0:T(256)S(1)} %get-tuple-element.7, f32[256]{0:T(256)S(1)} %pmax.7, f32[256]{0:T(256)S(1)} %copy-done.1), kind=kOutput, calls=%fused_computation | convolution fusion | flops 2157707264 | bytes 28315648 | tf_op jit(solution)/shard_map/dot_general | solution.py:38
  261.5 0.0 reduce-scatter.5.cloned.1.call-update
  261.5 0.0 reduce-scatter.3.cloned.1.call-start
  261.6 7.4 %convolution_convert_fusion = bf16[256,4096]{1,0:T(8,128)(2,1)} fusion(bf16[1024,4096]{1,0:T(8,128)(2,1)} %all-gather.4.cloned.1.call-done, f32[256,1024]{1,0:T(8,128)S(1)} %get-tuple-element.10, s32[256]{0:T(256)S(1)} %broadcast_subtract_fusion, f32[256]{0:T(256)S(1)} %get-tuple-element.7, f32[256]{0:T(256)S(1)} %pmax.7, f32[256]{0:T(256)S(1)} %copy-done.1), kind=kOutput, calls=%fused_computation.1 | convolution fusion | flops 2150367232 | bytes 11538432 | tf_op jit(solution)/shard_map/dot_general | solution.py:24
  268.9 0.0 reduce-scatter.3.cloned.1.call-update
  269.0 0.6 add_subtract_fusion.1
  269.5 56.1 %reduce-scatter.5.cloned.1.call-done = bf16[64,4096]{1,0:T(8,128)(2,1)} async-done(((bf16[1024,4096]{1,0:T(8,128)(2,1)}), bf16[64,4096]{1,0:T(8,128)(2,1)}) %reduce-scatter.5.cloned.1.call-update) | async-done | bytes 524304 | tf_op jit(solution)/shard_map/reduce_scatter | solution.py:41
  325.6 2.1 convert_element_type.20
  327.7 83.7 %reduce-scatter.3.cloned.1.call-done = bf16[256,256]{1,0:T(8,128)(2,1)} async-done(((bf16[256,4096]{1,0:T(8,128)(2,1)}), bf16[256,256]{1,0:T(8,128)(2,1)}) %reduce-scatter.3.cloned.1.call-update) | async-done | bytes 131088 | tf_op jit(solution)/shard_map/reduce_scatter | solution.py:25
  (4 shorter events, 0.0 us)
Async XLA Ops:
  7.2 163.1 %copy-start = (bf16[256,4096]{1,0:T(8,128)(2,1)S(1)}, bf16[256,4096]{1,0:T(8,128)(2,1)}, u32[]{:S(2)}) copy-start(bf16[256,4096]{1,0:T(8,128)(2,1)} %param.8) | copy-start | bytes 6291460
  7.2 55.8 %all-gather.6.cloned.1.call-start = ((), (), s32[]{:S(2)}) async-start(), calls=%async_computation.4 | async-start | bytes 2228224 | tf_op jit(solution)/shard_map/all_gather | solution.py:30
  7.9 106.9 %all-gather.8.cloned.1.call-start = ((), (), s32[]{:S(2)}) async-start(), calls=%async_computation.5 | async-start | bytes 2228224 | tf_op jit(solution)/shard_map/all_gather | solution.py:32
  8.7 161.5 %all-gather.4.cloned.1.call-start = ((), (), s32[]{:S(2)}) async-start(), calls=%async_computation.2 | async-start | bytes 8912896 | tf_op jit(solution)/shard_map/all_gather | solution.py:10
  9.4 316.2 %reduce-scatter.5.cloned.1.call-start = ((), (), s32[]{:S(2)}) async-start(), calls=%async_computation.6 | async-start | bytes 8912896 | tf_op jit(solution)/shard_map/reduce_scatter | solution.py:41
  125.1 127.2 %copy-start.1 = (f32[256]{0:T(256)S(1)}, f32[256]{0:T(256)}, u32[]{:S(2)}) copy-start(f32[256]{0:T(256)} %param.11) | copy-start | bytes 3076
  261.5 149.9 %reduce-scatter.3.cloned.1.call-start = ((), (), s32[]{:S(2)}) async-start(), calls=%async_computation.3 | async-start | bytes 2228224 | tf_op jit(solution)/shard_map/reduce_scatter | solution.py:25
Sparse Core Ops, SparseCore 0:
  10.4 52.5 all-gather.5
  65.5 49.3 all-gather.7
  116.7 53.4 all-gather.3
  261.6 63.9 reduce-scatter.4
  329.6 81.7 reduce-scatter.2
where the time goes:
time: 418 us
  waiting for transfers between devices  272 us (65%)
  blocking collectives  92.2 us (22%)
  matrix products  32.7 us (8%)
  between operations  14.5 us (3%)
    reduce_scatter x1, waiting for transfers between devices, shards(): lax.psum_scatter(state_term.astype(jnp.bfloat16), 'vocab', scatter_dimens...  83.7 us
    reduce_scatter x1, waiting for transfers between devices, shards(): lax.psum_scatter((head + looked_up).astype(jnp.bfloat16), 'dp', scatter_d...  56.1 us
    all_gather x1, waiting for transfers between devices, shards(): lax.all_gather(dec_cot, 'vocab', axis=0, tiled=True)  51.8 us
    all_gather x1, waiting for transfers between devices, shards(): gathered = lax.all_gather(table, 'dp', axis=0, tiled=True)  45.1 us
    pmax x1, blocking collectives, shards(): row_max = lax.pmax(local_max, 'vocab')  40.3 us
    psum x1, blocking collectives, shards(): lax.psum((jnp.sum(expo, axis=1), target_part), 'vocab')  35.5 us
    all_gather x1, waiting for transfers between devices, shards(): lax.all_gather(enc_cot, 'vocab', axis=0, tiled=True)  32.8 us
    unnamed x1, blocking collectives  16.5 us
  transfers between devices with their start and end apart: 5, of which 5 were waited for; matrix products, arithmetic and copies ran while one was open for 6% of the time, Pallas kernels for 0%

commit v1 on v0

--- a/solution.py
+++ b/solution.py
@@ -7,7 +7,15 @@
 def shards(hidden, table, targets, token_scale, enc_ids, enc_cot, dec_ids, dec_cot):
     vocab_rows = table.shape[0] * lax.axis_size("dp")
     offset = lax.axis_index("vocab") * vocab_rows
-    gathered = lax.all_gather(table, "dp", axis=0, tiled=True)
+    gathered = jnp.concatenate(
+        lax.all_to_all(
+            jnp.stack([table for _ in range(lax.axis_size("dp"))]),
+            axis_name="dp",
+            split_axis=0,
+            concat_axis=0,
+        ),
+        axis=0,
+    )
     logits = jnp.dot(hidden, gathered.T, preferred_element_type=jnp.float32)
     local_target = targets - offset
     columns = jnp.arange(vocab_rows, dtype=jnp.int32)

time: 418 us -> 452 us (1.081)
  waiting for transfers between devices: 272 us -> 294 us
  starting transfers between devices: 0.19 us -> 8.88 us
    all_to_all x0 -> x1, waiting for transfers between devices: none -> 65.8 us  [shards(): lax.all_to_all(jnp.stack([table for _ in range(lax.axis_size('dp'))]), ax...]
    all_gather x1 -> x0, waiting for transfers between devices: 45.1 us -> none  [shards(): gathered = lax.all_gather(table, 'dp', axis=0, tiled=True)]
    all_to_all x0 -> x1, starting transfers between devices: none -> 8.73 us  [shards(): lax.all_to_all(jnp.stack([table for _ in range(lax.axis_size('dp'))]), ax...]
    another operation x0 -> x1, local copies, waits for them, and re-layouts: none -> 5.47 us  [shards(): jnp.stack([table for _ in range(lax.axis_size('dp'))])]
  transfers between devices with their start and end apart: 5 -> 5, of which waited for: 5 -> 5; matrix products, arithmetic and copies ran while one was open for 6% -> 5% of each run, Pallas kernels for 0% -> 0%
where the time goes in v1:
time: 452 us
  waiting for transfers between devices  294 us (65%)
  blocking collectives  92.6 us (20%)
  matrix products  32.7 us (7%)
  between operations  14.5 us (3%)
  starting transfers between devices  8.88 us (2%)
  local copies, waits for them, and re-layouts  6.55 us (1%)
    reduce_scatter x1, waiting for transfers between devices, shards(): lax.psum_scatter(state_term.astype(jnp.bfloat16), 'vocab', scatter_dimens...  83.7 us
    all_to_all x1, waiting for transfers between devices, shards(): lax.all_to_all(jnp.stack([table for _ in range(lax.axis_size('dp'))]), ax...  65.8 us
    reduce_scatter x1, waiting for transfers between devices, shards(): lax.psum_scatter((head + looked_up).astype(jnp.bfloat16), 'dp', scatter_d...  56.1 us
    all_gather x1, waiting for transfers between devices, shards(): lax.all_gather(dec_cot, 'vocab', axis=0, tiled=True)  51.8 us
    pmax x1, blocking collectives, shards(): row_max = lax.pmax(local_max, 'vocab')  40.7 us
    psum x1, blocking collectives, shards(): lax.psum((jnp.sum(expo, axis=1), target_part), 'vocab')  35.5 us
    all_gather x1, waiting for transfers between devices, shards(): lax.all_gather(enc_cot, 'vocab', axis=0, tiled=True)  34.7 us
    unnamed x1, blocking collectives  16.5 us
  transfers between devices with their start and end apart: 5, of which 5 were waited for; matrix products, arithmetic and copies ran while one was open for 5% of the time, Pallas kernels for 0%

profile of v1, /device:TPU:32, one launch (start us, length us, event | category | flops | bytes accessed | tf_op | source)
XLA Modules:
  0.0 451.9 jit_solution(7261879827952441077)
XLA Ops:
  7.2 0.0 copy-start
  7.2 5.5 %stack.2 = bf16[16,64,4096]{2,1,0:T(8,128)(2,1)} broadcast(bf16[64,4096]{1,0:T(8,128)(2,1)} %param.9), dimensions={1,2} | broadcast | bytes 8912896 | tf_op jit(solution)/shard_map/stack | solution.py:12
  12.7 8.7 %all-to-all-start = ((bf16[16,64,4096]{2,1,0:T(8,128)(2,1)}), bf16[16,64,4096]{2,1,0:T(8,128)(2,1)}, u32[]{:S(2)}, u32[]{:S(2)}) async-start(bf16[16,64,4096]{2,1,0:T(8,128)(2,1)} %stack.2), calls=%async_computation | async-start | bytes 16777216 | tf_op jit(solution)/shard_map/all_to_all | solution.py:11
  21.4 0.0 all-gather.3.cloned.1.call-start
  21.4 0.7 all-gather.3.cloned.1.call-update
  22.1 0.0 all-gather.5.cloned.1.call-start
  22.2 0.7 all-gather.5.cloned.1.call-update
  22.9 0.0 reduce-scatter.5.cloned.1.call-start
  22.9 0.0 copy-done.5
  22.9 0.6 dynamic-slice
  24.2 0.0 copy-done.3
  24.2 0.2 dynamic-update-slice.1
  24.4 0.0 copy-done.4
  24.4 0.2 dynamic-update-slice
  24.7 16.5 %all-reduce.2 = (s32[256]{0:T(256)S(1)}, s32[256]{0:T(256)S(1)}) all-reduce(s32[256]{0:T(256)S(1)} %dynamic-update-slice.1, s32[256]{0:T(256)S(1)} %dynamic-update-slice), channel_id=1, replica_groups=mesh['dp'=16,'vocab'=16] {'vocab'}, use_global_device_ids=true, to_apply=%add.1 | all-reduce | flops 512 | bytes 4096
  41.1 34.7 %all-gather.3.cloned.1.call-done = bf16[256,4096]{1,0:T(8,128)(2,1)} async-done(((bf16[16,4096]{1,0:T(8,128)(2,1)}), bf16[256,4096]{1,0:T(8,128)(2,1)}) %all-gather.3.cloned.1.call-update) | async-done | bytes 2097168 | tf_op jit(solution)/shard_map/all_gather | solution.py:38
  75.9 51.8 %all-gather.5.cloned.1.call-done = bf16[256,4096]{1,0:T(8,128)(2,1)} async-done(((bf16[16,4096]{1,0:T(8,128)(2,1)}), bf16[256,4096]{1,0:T(8,128)(2,1)}) %all-gather.5.cloned.1.call-update) | async-done | bytes 2097168 | tf_op jit(solution)/shard_map/all_gather | solution.py:40
  127.7 10.3 %fusion = f32[1024,4096]{1,0:T(8,128)} fusion(bf16[256,4096]{1,0:T(8,128)(2,1)} %all-gather.5.cloned.1.call-done, bf16[256,4096]{1,0:T(8,128)(2,1)} %all-gather.3.cloned.1.call-done, s32[512]{0:T(512)S(1)} %add_subtract_fusion), kind=kOutput, calls=%fused_computation.2 | convolution fusion | flops 4303880192 | bytes 20973568 | tf_op jit(solution)/shard_map/dot_general | solution.py:45
  138.0 65.8 %all-to-all-done = bf16[16,64,4096]{2,1,0:T(8,128)(2,1)} async-done(((bf16[16,64,4096]{2,1,0:T(8,128)(2,1)}), bf16[16,64,4096]{2,1,0:T(8,128)(2,1)}, u32[]{:S(2)}, u32[]{:S(2)}) %all-to-all-start) | async-done | bytes 8388640 | tf_op jit(solution)/shard_map/all_to_all | solution.py:11
  203.8 5.8 %fusion.7 = (f32[256]{0:T(256)S(1)}, f32[256,1024]{1,0:T(8,128)S(1)}) fusion(bf16[256,4096]{1,0:T(8,128)(2,1)S(1)} %copy-done, bf16[1024,4096]{1,0:T(8,128)(2,1)} %bitcast), kind=kOutput, calls=%fused_computation.17 | convolution fusion | flops 2147745536 | bytes 11535360 | tf_op jit(solution)/shard_map/dot_general | solution.py:19
  209.6 40.7 %pmax.7 = f32[256]{0:T(256)S(1)} all-reduce(f32[256]{0:T(256)S(1)} %get-tuple-element.9), channel_id=1, replica_groups=mesh['dp'=16,'vocab'=16] {'vocab'}, use_global_device_ids=true, to_apply=%region_1.2 | all-reduce | flops 256 | bytes 2048 | tf_op jit(solution)/shard_map/pmax | solution.py:25
  250.3 0.5 select_reduce_fusion
  250.8 35.5 %all-reduce.3 = (f32[256]{0:T(256)S(1)}, f32[256]{0:T(256)S(1)}) all-reduce(f32[256]{0:T(256)S(1)} %get-tuple-element.4, f32[256]{0:T(256)S(1)} %get-tuple-element.3), channel_id=1, replica_groups=mesh['dp'=16,'vocab'=16] {'vocab'}, use_global_device_ids=true, to_apply=%region_3.4 | all-reduce | flops 512 | bytes 4096 | tf_op jit(solution)/shard_map/psum | solution.py:27
  286.2 9.2 %add_convert_fusion = bf16[1024,4096]{1,0:T(8,128)(2,1)} fusion(f32[1024,4096]{1,0:T(8,128)} %fusion, bf16[256,4096]{1,0:T(8,128)(2,1)S(1)} %copy-done, f32[256,1024]{1,0:T(8,128)S(1)} %get-tuple-element.10, s32[256]{0:T(256)S(1)} %broadcast_subtract_fusion, f32[256]{0:T(256)S(1)} %get-tuple-element.7, f32[256]{0:T(256)S(1)} %pmax.7, f32[256]{0:T(256)S(1)} %copy-done.1), kind=kOutput, calls=%fused_computation | convolution fusion | flops 2157707264 | bytes 28315648 | tf_op jit(solution)/shard_map/dot_general | solution.py:46
  295.4 0.0 reduce-scatter.5.cloned.1.call-update
  295.5 0.0 reduce-scatter.3.cloned.1.call-start
  295.5 7.4 %convolution_convert_fusion = bf16[256,4096]{1,0:T(8,128)(2,1)} fusion(bf16[1024,4096]{1,0:T(8,128)(2,1)} %bitcast, f32[256,1024]{1,0:T(8,128)S(1)} %get-tuple-element.10, s32[256]{0:T(256)S(1)} %broadcast_subtract_fusion, f32[256]{0:T(256)S(1)} %get-tuple-element.7, f32[256]{0:T(256)S(1)} %pmax.7, f32[256]{0:T(256)S(1)} %copy-done.1), kind=kOutput, calls=%fused_computation.1 | convolution fusion | flops 2150367232 | bytes 11538432 | tf_op jit(solution)/shard_map/dot_general | solution.py:32
  302.9 0.0 reduce-scatter.3.cloned.1.call-update
  302.9 0.6 add_subtract_fusion.1
  303.5 56.1 %reduce-scatter.5.cloned.1.call-done = bf16[64,4096]{1,0:T(8,128)(2,1)} async-done(((bf16[1024,4096]{1,0:T(8,128)(2,1)}), bf16[64,4096]{1,0:T(8,128)(2,1)}) %reduce-scatter.5.cloned.1.call-update) | async-done | bytes 524304 | tf_op jit(solution)/shard_map/reduce_scatter | solution.py:49
  359.6 2.1 convert_element_type.20
  361.7 83.7 %reduce-scatter.3.cloned.1.call-done = bf16[256,256]{1,0:T(8,128)(2,1)} async-done(((bf16[256,4096]{1,0:T(8,128)(2,1)}), bf16[256,256]{1,0:T(8,128)(2,1)}) %reduce-scatter.3.cloned.1.call-update) | async-done | bytes 131088 | tf_op jit(solution)/shard_map/reduce_scatter | solution.py:33
  (12 shorter events, 0.0 us)
Async XLA Ops:
  7.2 196.6 %copy-start = (bf16[256,4096]{1,0:T(8,128)(2,1)S(1)}, bf16[256,4096]{1,0:T(8,128)(2,1)}, u32[]{:S(2)}) copy-start(bf16[256,4096]{1,0:T(8,128)(2,1)} %param.8) | copy-start | bytes 6291460
  12.6 10.3 %copy-start.5 = (u32[256]{0:T(256)S(1)}, u32[256]{0:T(256)}, u32[]{:S(2)}) copy-start(u32[256]{0:T(256)} %constant.17) | copy-start | bytes 3076
  12.6 11.5 %copy-start.3 = (s32[16]{0:T(128)S(1)}, s32[16]{0:T(128)}, u32[]{:S(2)}) copy-start(s32[16]{0:T(128)} %param.14) | copy-start | bytes 196
  12.7 11.8 %copy-start.4 = (s32[16]{0:T(128)S(1)}, s32[16]{0:T(128)}, u32[]{:S(2)}) copy-start(s32[16]{0:T(128)} %param.12) | copy-start | bytes 196
  12.7 28.5 %copy-start.2 = (s32[256]{0:T(256)S(1)}, s32[256]{0:T(256)}, u32[]{:S(2)}) copy-start(s32[256]{0:T(256)} %param.10) | copy-start | bytes 3076
  12.7 191.1 %all-to-all-start = ((bf16[16,64,4096]{2,1,0:T(8,128)(2,1)}), bf16[16,64,4096]{2,1,0:T(8,128)(2,1)}, u32[]{:S(2)}, u32[]{:S(2)}) async-start(bf16[16,64,4096]{2,1,0:T(8,128)(2,1)} %stack.2), calls=%async_computation | async-start | bytes 16777216 | tf_op jit(solution)/shard_map/all_to_all | solution.py:11
  21.4 54.5 %all-gather.3.cloned.1.call-start = ((), (), s32[]{:S(2)}) async-start(), calls=%async_computation.4 | async-start | bytes 2228224 | tf_op jit(solution)/shard_map/all_gather | solution.py:38
  22.1 105.6 %all-gather.5.cloned.1.call-start = ((), (), s32[]{:S(2)}) async-start(), calls=%async_computation.5 | async-start | bytes 2228224 | tf_op jit(solution)/shard_map/all_gather | solution.py:40
  22.9 336.7 %reduce-scatter.5.cloned.1.call-start = ((), (), s32[]{:S(2)}) async-start(), calls=%async_computation.6 | async-start | bytes 8912896 | tf_op jit(solution)/shard_map/reduce_scatter | solution.py:49
  203.8 82.4 %copy-start.1 = (f32[256]{0:T(256)S(1)}, f32[256]{0:T(256)}, u32[]{:S(2)}) copy-start(f32[256]{0:T(256)} %param.11) | copy-start | bytes 3076
  295.5 149.9 %reduce-scatter.3.cloned.1.call-start = ((), (), s32[]{:S(2)}) async-start(), calls=%async_computation.3 | async-start | bytes 2228224 | tf_op jit(solution)/shard_map/reduce_scatter | solution.py:33
Sparse Core Ops, SparseCore 0:
  24.7 51.1 all-gather.2
  78.3 49.3 all-gather.4
  295.6 63.9 reduce-scatter.4
  363.6 81.7 reduce-scatter.2
